TPU v7x, 128 devices: a whole 4x4x4 slice. The times are simulated.
128 devices in a mesh: dp: 4 (over y), ctx: 32 (over z, x, core).
Axes of the slice: x: 4, y: 4, z: 4, core: 2. Of those that a mesh axis runs over, the one named last changes fastest.
Arguments:
- projected: bfloat16 [4, 4096, 3, 8192], P('dp', 'ctx'), may hold values from -6 to 6
- short_filter: float32 [3, 7, 8192], replicated, may hold values from -2.4 to 2.4
- residues: float32 [512, 16], replicated, may hold values from -0.06 to 0.06
- decay_rates: float32 [512, 16], replicated, may hold values from 2.4414063e-05 to 0.03125
- skip_gain: float32 [8192], replicated, may hold values from 0.5 to 1.5
- cotangent: bfloat16 [4, 4096, 8192], P('dp', 'ctx'), may hold values from -6 to 6
Outputs:
- output: bfloat16 [4, 4096, 8192], P('dp', 'ctx')
- grad_projected: bfloat16 [4, 4096, 3, 8192], P('dp', 'ctx')
- grad_short: float32 [3, 7, 8192], replicated
- grad_skip: float32 [8192], replicated
All inputs are finite; a program needn't handle non-finite values.
Results may differ from a plain program's by a relative error of at most 0.001.
Values may be sent and summed in bfloat16 or wider, within the bound.
A program may use at most 320 MiB of HBM per device.

v0:
```python
import jax
import jax.numpy as jnp
from jax import lax
from jax.sharding import PartitionSpec as P

BLK = 64
HIGHEST = lax.Precision.HIGHEST


def passed_along(value, axis, steps):
    count = lax.axis_size(axis)
    first, last = (max(0, -steps), min(count, count - steps))
    return lax.ppermute(value, axis, [(source, source + steps) for source in range(first, last)])


def edge_tables(residues, decay_rates, span):
    offsets = jnp.arange(span).astype(jnp.float32)
    carry_fwd = residues[:, None, :] * jnp.exp(
        -decay_rates[:, None, :] * (offsets[None, :, None] + 1.0)
    )
    carry_bwd = residues[:, None, :] * jnp.exp(
        -decay_rates[:, None, :] * (span - offsets)[None, :, None]
    )
    decay_factor = jnp.exp(-decay_rates * span)
    return (carry_fwd, carry_bwd, decay_factor)


def block_tables(residues, decay_rates, block_rows):
    offsets = jnp.arange(block_rows).astype(jnp.float32)
    powers = jnp.exp(-decay_rates[:, :, None] * offsets[None, None, :])
    lag_filter = jnp.sum(residues[:, :, None] * powers, axis=1)
    lag_index = jnp.arange(block_rows)[:, None] - jnp.arange(block_rows)[None, :]
    toeplitz = jnp.where(lag_index >= 0, lag_filter[:, jnp.maximum(lag_index, 0)], 0.0)
    carry_fwd, carry_bwd, decay_factor = edge_tables(residues, decay_rates, block_rows)
    return (toeplitz, powers[:, :, ::-1], powers, carry_fwd, carry_bwd, decay_factor)


def forward_local(inputs, tables):
    toeplitz, end_weights, start_weights, carry_fwd, carry_bwd, decay_factor = tables
    local_out = jnp.einsum("gts,bkswg->bktwg", toeplitz, inputs, precision=HIGHEST)
    block_ends = jnp.einsum("gns,bkswg->bknwg", end_weights, inputs, precision=HIGHEST)
    factor = decay_factor.T[:, None, :]

    def forward_advance(carried, block_term):
        return (factor * carried + block_term, carried)

    final_state, entering = lax.scan(
        forward_advance, jnp.zeros_like(block_ends[:, 0]), jnp.moveaxis(block_ends, 1, 0)
    )
    entering = jnp.moveaxis(entering, 0, 1)
    local_out = local_out + jnp.einsum("gjn,bknwg->bkjwg", carry_fwd, entering, precision=HIGHEST)
    return (local_out, final_state)


def backward_local(grads, tables):
    toeplitz, end_weights, start_weights, carry_fwd, carry_bwd, decay_factor = tables
    local_grad = jnp.einsum("gts,bktwg->bkswg", toeplitz, grads, precision=HIGHEST)
    block_starts = jnp.einsum("gnt,bktwg->bknwg", start_weights, grads, precision=HIGHEST)
    factor = decay_factor.T[:, None, :]

    def backward_advance(carried, block_term):
        return (factor * carried + block_term, carried)

    final_adjoint, following = lax.scan(
        backward_advance,
        jnp.zeros_like(block_starts[:, 0]),
        jnp.moveaxis(block_starts, 1, 0),
        reverse=True,
    )
    following = jnp.moveaxis(following, 0, 1)
    local_grad = local_grad + jnp.einsum(
        "gsn,bknwg->bkswg", carry_bwd, following, precision=HIGHEST
    )
    return (local_grad, final_adjoint)


def short_conv(padded, short_filter, count):
    tap_count = short_filter.shape[1]
    total = jnp.zeros((padded.shape[0], count) + padded.shape[2:], jnp.float32)
    for offset in range(tap_count):
        begin = tap_count - 1 - offset
        total = total + short_filter[:, offset, :] * padded[:, begin : begin + count].astype(
            jnp.float32
        )
    return total


def short_conv_grad(ahead, short_filter, count):
    tap_count = short_filter.shape[1]
    total = jnp.zeros((ahead.shape[0], count) + ahead.shape[2:], jnp.float32)
    for offset in range(tap_count):
        total = total + short_filter[:, offset, :] * ahead[:, offset : offset + count]
    return total


def filter_grad(grad_mixed, padded, tap_count, count):
    products = jnp.stack(
        [
            grad_mixed
            * padded[:, tap_count - 1 - offset : tap_count - 1 - offset + count].astype(jnp.float32)
            for offset in range(tap_count)
        ],
        axis=3,
    )
    return jnp.sum(products, axis=(0, 1))


def chains(local_end, local_adjoint, factor):
    wide_factor = factor[:, None, :]

    def forward_turn(turn_index, incoming):
        return passed_along(wide_factor * incoming + local_end, "ctx", 1)

    def backward_turn(turn_index, incoming):
        return passed_along(wide_factor * incoming + local_adjoint, "ctx", -1)

    entering = lax.fori_loop(0, lax.axis_size("ctx") - 1, forward_turn, jnp.zeros_like(local_end))
    arriving = lax.fori_loop(
        0, lax.axis_size("ctx") - 1, backward_turn, jnp.zeros_like(local_adjoint)
    )
    return (entering, arriving)


def local(projected, short_filter, residues, decay_rates, skip_gain, cotangent):
    batch_size = projected.shape[0]
    local_rows = projected.shape[1]
    channels = projected.shape[3]
    tap_count = short_filter.shape[1]
    filter_groups = residues.shape[0]
    group_width = channels // filter_groups
    previous = passed_along(projected[:, local_rows - (tap_count - 1) :], "ctx", 1)
    padded = jnp.concatenate([previous, projected], axis=1)
    mixed = short_conv(padded, short_filter, local_rows)
    query_part = mixed[:, :, 0]
    key_part = mixed[:, :, 1]
    value_part = mixed[:, :, 2]
    gated = key_part * value_part
    tables = block_tables(residues, decay_rates, BLK)
    carry_fwd, carry_bwd, decay_device = edge_tables(residues, decay_rates, local_rows)
    device_factor = decay_device.T
    block_shape = (batch_size, local_rows // BLK, BLK, group_width, filter_groups)
    conv_out, local_end = forward_local(gated.reshape(block_shape), tables)
    upstream = cotangent.astype(jnp.float32)
    grad_filtered = upstream * query_part
    conv_grad, local_adjoint = backward_local(grad_filtered.reshape(block_shape), tables)
    entering, arriving = chains(local_end, local_adjoint, device_factor)
    carried = jnp.einsum("gtn,bnwg->btwg", carry_fwd, entering, precision=HIGHEST)
    filtered = conv_out.reshape(gated.shape) + carried.reshape(gated.shape) + skip_gain * gated
    output = (query_part * filtered).astype(jnp.bfloat16)
    grad_query = upstream * filtered
    returned = jnp.einsum("gsn,bnwg->bswg", carry_bwd, arriving, precision=HIGHEST)
    grad_gated = (
        conv_grad.reshape(gated.shape) + returned.reshape(gated.shape) + skip_gain * grad_filtered
    )
    grad_mixed = jnp.stack([grad_query, grad_gated * value_part, grad_gated * key_part], axis=2)
    following = passed_along(grad_mixed[:, : tap_count - 1], "ctx", -1)
    ahead = jnp.concatenate([grad_mixed, following], axis=1)
    grad_projected = short_conv_grad(ahead, short_filter, local_rows).astype(jnp.bfloat16)
    short_local = filter_grad(grad_mixed, padded, tap_count, local_rows)
    skip_local = jnp.sum(grad_filtered * gated, axis=(0, 1))
    grad_short, grad_skip = lax.psum((short_local, skip_local), ("dp", "ctx"))
    return (output, grad_projected, grad_short, grad_skip)


def solution(mesh):
    placed = (P("dp", "ctx", None, None), P(), P(), P(), P(), P("dp", "ctx", None))
    return jax.shard_map(
        local,
        mesh=mesh,
        in_specs=placed,
        out_specs=(P("dp", "ctx", None), P("dp", "ctx", None, None), P(), P()),
        check_vma=False,
    )
```

profile of v0, /device:TPU:1, one launch (start us, length us, event | category | flops | bytes accessed | tf_op | source)
XLA Modules:
  0.0 1422.1 jit_solution(7022299706834155832)
XLA Ops:
  33.3 16.8 %gather_fusion = f32[4096,512]{1,0:T(8,128)} fusion(f32[512,64]{0,1:T(8,128)S(1)} %copy.52, s32[4096]{0:T(1024)S(1)} %broadcast_clamp_fusion), kind=kCustom, calls=%fused_computation | custom fusion | bytes 16793600 | tf_op jit(solution)/shard_map/gather | solution.py:33
  50.1 16.2 %copy.53 = f32[64,64,512]{1,0,2:T(8,128)} copy(f32[64,64,512]{2,1,0:T(8,128)} %bitcast.190) | data formatting | bytes 16777216 | tf_op jit(solution)/shard_map/gather | solution.py:33
  66.9 18.8 %fusion.11 = f32[1,128,3,8192]{3,1,2,0:T(8,128)S(1)} fusion(bf16[1,128,3,8192]{3,1,2,0:T(8,128)(2,1)} %param.14, bf16[1,6,3,8192]{3,1,2,0:T(8,128)(2,1)S(1)} %collective-permute-done.2, f32[3,8192]{1,0:T(4,128)S(1)} %get-tuple-element.314, f32[3,8192]{1,0:T(4,128)S(1)} %get-tuple-element.315, f32[3,8192]{1,0:T(4,128)S(1)} %get-tuple-element.316, ...), kind=kLoop, calls=%fused_computation.38 | loop fusion | flops 119537664 | bytes 19857408 | tf_op jit(solution)/shard_map/add | solution.py:82
  101.1 13.1 fusion.67
  127.8 29.5 %fusion.2 = f32[512,2,16,64]{3,2,1,0:T(8,128)S(1)} fusion(f32[2,64,16,512]{1,2,0,3:T(8,128)} %copy.54, f32[64,64,512]{1,0,2:T(8,128)} %copy.53, pred[64,64]{1,0:T(8,128)(4,1)S(1)} %subtract_compare_fusion), kind=kOutput, calls=%fused_computation.9 | convolution fusion | flops 807403520 | bytes 16781312 | tf_op jit(solution)/shard_map/gts,bkswg->bktwg/dot_general | solution.py:40
  157.3 11.3 add_bitcast_fusion.1
  181.3 353.5 %while.50 = (s32[]{:T(128)}, f32[1,16,16,512]{3,2,1,0:T(8,128)S(1)}, f32[16,512]{1,0:T(8,128)S(1)}, f32[1,16,16,512]{3,2,1,0:T(8,128)S(1)}, s32[]{:T(128)}) while((s32[]{:T(128)}, f32[1,16,16,512]{3,2,1,0:T(8,128)S(1)}, f32[16,512]{1,0:T(8,128)S(1)}, f32[1,16,16,512]{3,2,1,0:T(8,128)S(1)}, s32[]{:T(128)}) %tuple.113), condition=%wide.region_4.5_spmd, body=%wide.region_3.4_spmd.sunk | while | flops 262146 | bytes 3702885 | solution.py:117
  555.1 13.5 multiply_reduce_fusion
  584.9 12.2 fusion.72
  597.1 19.1 %fusion = f32[512,2,16,64]{3,2,1,0:T(8,128)} fusion(f32[2,64,16,512]{1,2,0,3:T(8,128)S(1)} %copy-done.5, f32[64,64,512]{1,0,2:T(8,128)} %copy.53, pred[64,64]{1,0:T(8,128)(4,1)S(1)} %subtract_compare_fusion), kind=kOutput, calls=%fused_computation.7 | convolution fusion | flops 807403520 | bytes 16781312 | tf_op jit(solution)/shard_map/gts,bktwg->bkswg/dot_general | solution.py:57
  630.3 13.7 add_bitcast_fusion
  656.7 397.2 %while.51 = (s32[]{:T(128)}, f32[1,16,16,512]{3,2,1,0:T(8,128)S(1)}, f32[16,512]{1,0:T(8,128)S(1)}, f32[1,16,16,512]{3,2,1,0:T(8,128)S(1)}, s32[]{:T(128)}) while((s32[]{:T(128)}, f32[1,16,16,512]{3,2,1,0:T(8,128)S(1)}, f32[16,512]{1,0:T(8,128)S(1)}, f32[1,16,16,512]{3,2,1,0:T(8,128)S(1)}, s32[]{:T(128)}) %tuple.125), condition=%wide.region_8.9_spmd, body=%wide.region_7.8_spmd.sunk | while | flops 262146 | bytes 3702885 | solution.py:118
  658.8 11.4 collective-permute-done.1
  684.8 11.4 collective-permute-done.1
  710.9 11.4 collective-permute-done.1
  737.0 11.4 collective-permute-done.1
  750.5 10.7 collective-permute-done.1
  1074.3 10.8 fusion.51
  1094.9 10.9 fusion.13
  1119.3 11.2 fusion.15
  1157.5 27.9 %reduce_sum.28 = f32[3,7,8192]{2,0,1:T(4,128)} reduce(f32[1,128,3,7,8192]{4,1,2,3,0:T(8,128)} %fusion.25, f32[]{:T(128)} %constant.65.clone.1), dimensions={0,1}, to_apply=%region_9.10 | reduce | flops 21848064 | bytes 88768512 | tf_op jit(solution)/shard_map/reduce_sum | solution.py:105
  1185.5 102.3 %psum.15 = f32[8192]{0:T(1024)} all-reduce(f32[8192]{0:T(1024)S(1)} %copy-done.25), channel_id=1, replica_groups=mesh['dp'=4,'ctx'=32] {'dp','ctx'}, use_global_device_ids=true, to_apply=%region_12.13 | all-reduce | flops 8192 | bytes 65536 | tf_op jit(solution)/shard_map/psum | solution.py:161
  1287.8 80.9 %all-reduce.2.cloned.1.call-done = f32[3,7,8192]{2,0,1:T(4,128)} async-done(((f32[3,7,8192]{2,0,1:T(4,128)}), f32[3,7,8192]{2,0,1:T(4,128)}) %all-reduce.2.cloned.1.call-update) | async-done | bytes 688144 | tf_op jit(solution)/shard_map/psum | solution.py:161
  1381.5 33.6 %fusion.27 = bf16[1,128,3,8192]{3,1,2,0:T(8,128)(2,1)} fusion(f32[1,134,3,8192]{3,1,2,0:T(8,128)} %pad_maximum_fusion, f32[3,8192]{1,0:T(4,128)S(1)} %copy-done.13, f32[3,8192]{1,0:T(4,128)S(1)} %copy-done.15, f32[3,8192]{1,0:T(4,128)S(1)} %copy-done.17, f32[3,8192]{1,0:T(4,128)S(1)} %copy-done.19, f32[3,8192]{1,0:T(4,128)S(1)} %copy-done.21, ...), kind=kLoop, calls=%fused_computation.55 | loop fusion | flops 50331648 | bytes 95059968 | tf_op jit(solution)/shard_map/convert_element_type | solution.py:158
  (314 shorter events, 908.8 us)
Async XLA Ops:
  7.2 1361.6 %all-reduce.2.cloned.1.call-start = ((), (), s32[]{:S(2)}) async-start(), calls=%async_computation | async-start | bytes 1835008 | tf_op jit(solution)/shard_map/psum | solution.py:161
  8.3 58.6 %collective-permute-start.2 = (bf16[1,6,3,8192]{3,1,2,0:T(8,128)(2,1)S(1)}, bf16[1,6,3,8192]{3,1,2,0:T(8,128)(2,1)S(1)}, u32[]{:S(2)}, u32[]{:S(2)}) collective-permute-start(bf16[1,6,3,8192]{3,1,2,0:T(8,128)(2,1)S(1)} %slice.87), channel_id=1, source_target_pairs={{0,1},{1,2},{2,3},{3,4},{4,5},{5,6},{6,7},{7,8},{8,9},{9,10},{10,1... | collective-permute-start | bytes 884744 | tf_op jit(solution)/shard_map/ppermute | solution.py:13
  382.2 12.6 collective-permute-start
  395.0 12.6 collective-permute-start
  407.7 12.6 collective-permute-start
  420.4 12.6 collective-permute-start
  433.1 12.6 collective-permute-start
  445.9 12.6 collective-permute-start
  458.6 12.6 collective-permute-start
  471.3 12.6 collective-permute-start
  484.1 12.6 collective-permute-start
  496.8 12.6 collective-permute-start
  509.5 12.6 collective-permute-start
  522.2 12.6 collective-permute-start
  656.8 13.4 collective-permute-start.1
  682.9 13.4 collective-permute-start.1
  709.0 13.4 collective-permute-start.1
  735.1 13.4 collective-permute-start.1
  748.5 12.6 collective-permute-start.1
  774.0 12.6 collective-permute-start.1
  786.7 12.6 collective-permute-start.1
  799.5 12.6 collective-permute-start.1
  812.2 12.6 collective-permute-start.1
  1117.0 254.2 %collective-permute-start.3 = (f32[1,6,3,8192]{3,0,2,1:T(1,128)S(1)}, f32[1,6,3,8192]{3,0,2,1:T(1,128)S(1)}, u32[]{:S(2)}, u32[]{:S(2)}) collective-permute-start(f32[1,6,3,8192]{3,0,2,1:T(1,128)S(1)} %copy.74), channel_id=1, source_target_pairs={{1,0},{2,1},{3,2},{4,3},{5,4},{6,5},{7,6},{8,7},{9,8},{10,9},{11,1... | collective-permute-start | bytes 1769480 | tf_op jit(solution)/shard_map/ppermute | solution.py:13
  (69 other events, 898.7 us)
Sparse Core Ops, SparseCore 0:
  1185.6 183.0 all-reduce.1
where the time goes:
time: 1430 us; the launch traced here: 1420 us
  waiting for transfers between devices  604 us (42%)
  starting transfers between devices  227 us (16%)
  other arithmetic  199 us (14%)
  local copies, waits for them, and re-layouts  160 us (11%)
  matrix products  114 us (8%)
  blocking collectives  102 us (7%)
  between operations  14.9 us (1%)
    ppermute x64, waiting for transfers between devices, passed_along(): lax.ppermute(value, axis, [(source, source + steps) for source in range(f...  523 us
    ppermute x64, starting transfers between devices, passed_along(): lax.ppermute(value, axis, [(source, source + steps) for source in range(f...  227 us
    psum x1, blocking collectives, local(): grad_short, grad_skip = lax.psum((short_local, skip_local), ('dp', 'ctx'))  102 us
    psum x1, waiting for transfers between devices, local(): grad_short, grad_skip = lax.psum((short_local, skip_local), ('dp', 'ctx'))  80.9 us
    unnamed x9, other arithmetic  43.6 us
    convert_element_type x1, other arithmetic, local(): short_conv_grad(ahead, short_filter, local_rows).astype(jnp.bfloat16)  33.6 us
    gather x2, local copies, waits for them, and re-layouts, block_tables(): lag_filter[:, jnp.maximum(lag_index, 0)]  33.1 us
    another operation x9, local copies, waits for them, and re-layouts  32 us
  transfers between devices with their start and end apart: 65, of which 63 were waited for; matrix products, arithmetic and copies ran while one was open for 9% of the time, Pallas kernels for 0%

commit v1 on v0

--- a/solution.py
+++ b/solution.py
@@ -158,7 +158,7 @@
     grad_projected = short_conv_grad(ahead, short_filter, local_rows).astype(jnp.bfloat16)
     short_local = filter_grad(grad_mixed, padded, tap_count, local_rows)
     skip_local = jnp.sum(grad_filtered * gated, axis=(0, 1))
-    grad_short, grad_skip = lax.psum((short_local, skip_local), ("dp", "ctx"))
+    grad_short, grad_skip = lax.psum(lax.psum((short_local, skip_local), "ctx"), "dp")
     return (output, grad_projected, grad_short, grad_skip)
 
 

time: 1430 us -> 1420 us (level)
  waiting for transfers between devices: 604 us -> 525 us
  blocking collectives: 102 us -> 157 us
    psum x1 -> x2, waiting for transfers between devices: 80.9 us -> 2.56 us  [the longest x1 2.56 us: local(): lax.psum(lax.psum((short_local, skip_local), 'ctx'), 'dp')]
    psum x1 -> x2, blocking collectives: 102 us -> 157 us  [the longest x1 142 us: local(): lax.psum((short_local, skip_local), 'ctx')]
  transfers between devices with their start and end apart: 65 -> 66, of which waited for: 63 -> 63; matrix products, arithmetic and copies ran while one was open for 9% -> 12% of each run, Pallas kernels for 0% -> 0%
where the time goes in v1:
time: 1420 us; the launch traced here: 1400 us
  waiting for transfers between devices  525 us (37%)
  starting transfers between devices  227 us (16%)
  other arithmetic  200 us (14%)
  local copies, waits for them, and re-layouts  160 us (11%)
  blocking collectives  157 us (11%)
  matrix products  114 us (8%)
  between operations  15.2 us (1%)
    ppermute x64, waiting for transfers between devices, passed_along(): lax.ppermute(value, axis, [(source, source + steps) for source in range(f...  523 us
    ppermute x64, starting transfers between devices, passed_along(): lax.ppermute(value, axis, [(source, source + steps) for source in range(f...  227 us
    psum x1, blocking collectives, local(): lax.psum((short_local, skip_local), 'ctx')  142 us
    unnamed x9, other arithmetic  44.1 us
    convert_element_type x1, other arithmetic, local(): short_conv_grad(ahead, short_filter, local_rows).astype(jnp.bfloat16)  34.2 us
    gather x2, local copies, waits for them, and re-layouts, block_tables(): lag_filter[:, jnp.maximum(lag_index, 0)]  33.2 us
    another operation x9, local copies, waits for them, and re-layouts  32 us
    another operation x3, other arithmetic, local(): jnp.stack([grad_query, grad_gated * value_part, grad_gated * key_part], a...  30 us
  transfers between devices with their start and end apart: 66, of which 63 were waited for; matrix products, arithmetic and copies ran while one was open for 12% of the time, Pallas kernels for 0%

profile of v1, /device:TPU:1, one launch (start us, length us, event | category | flops | bytes accessed | tf_op | source)
XLA Modules:
  0.0 1399.7 jit_solution(12196109264308850510)
XLA Ops:
  33.3 16.9 %gather_fusion = f32[4096,512]{1,0:T(8,128)} fusion(f32[512,64]{0,1:T(8,128)S(1)} %copy.52, s32[4096]{0:T(1024)S(1)} %broadcast_clamp_fusion), kind=kCustom, calls=%fused_computation | custom fusion | bytes 16793600 | tf_op jit(solution)/shard_map/gather | solution.py:33
  50.2 16.3 %copy.53 = f32[64,64,512]{1,0,2:T(8,128)} copy(f32[64,64,512]{2,1,0:T(8,128)} %bitcast.190) | data formatting | bytes 16777216 | tf_op jit(solution)/shard_map/gather | solution.py:33
  67.0 18.8 %fusion.11 = f32[1,128,3,8192]{3,1,2,0:T(8,128)S(1)} fusion(bf16[1,128,3,8192]{3,1,2,0:T(8,128)(2,1)} %param.14, bf16[1,6,3,8192]{3,1,2,0:T(8,128)(2,1)S(1)} %collective-permute-done.2, f32[3,8192]{1,0:T(4,128)S(1)} %get-tuple-element.314, f32[3,8192]{1,0:T(4,128)S(1)} %get-tuple-element.315, f32[3,8192]{1,0:T(4,128)S(1)} %get-tuple-element.316, ...), kind=kLoop, calls=%fused_computation.38 | loop fusion | flops 119537664 | bytes 19857408 | tf_op jit(solution)/shard_map/add | solution.py:82
  101.2 12.9 fusion.67
  127.7 29.5 %fusion.2 = f32[512,2,16,64]{3,2,1,0:T(8,128)S(1)} fusion(f32[2,64,16,512]{1,2,0,3:T(8,128)} %copy.54, f32[64,64,512]{1,0,2:T(8,128)} %copy.53, pred[64,64]{1,0:T(8,128)(4,1)S(1)} %subtract_compare_fusion), kind=kOutput, calls=%fused_computation.9 | convolution fusion | flops 807403520 | bytes 16781312 | tf_op jit(solution)/shard_map/gts,bkswg->bktwg/dot_general | solution.py:40
  157.2 11.6 add_bitcast_fusion.1
  181.4 353.5 %while.50 = (s32[]{:T(128)}, f32[1,16,16,512]{3,2,1,0:T(8,128)S(1)}, f32[16,512]{1,0:T(8,128)S(1)}, f32[1,16,16,512]{3,2,1,0:T(8,128)S(1)}, s32[]{:T(128)}) while((s32[]{:T(128)}, f32[1,16,16,512]{3,2,1,0:T(8,128)S(1)}, f32[16,512]{1,0:T(8,128)S(1)}, f32[1,16,16,512]{3,2,1,0:T(8,128)S(1)}, s32[]{:T(128)}) %tuple.113), condition=%wide.region_4.5_spmd, body=%wide.region_3.4_spmd.sunk | while | flops 262146 | bytes 3702885 | solution.py:117
  555.1 13.5 multiply_reduce_fusion
  584.9 12.2 fusion.72
  597.2 19.1 %fusion = f32[512,2,16,64]{3,2,1,0:T(8,128)} fusion(f32[2,64,16,512]{1,2,0,3:T(8,128)S(1)} %copy-done.5, f32[64,64,512]{1,0,2:T(8,128)} %copy.53, pred[64,64]{1,0:T(8,128)(4,1)S(1)} %subtract_compare_fusion), kind=kOutput, calls=%fused_computation.7 | convolution fusion | flops 807403520 | bytes 16781312 | tf_op jit(solution)/shard_map/gts,bktwg->bkswg/dot_general | solution.py:57
  630.2 13.7 add_bitcast_fusion
  656.6 397.2 %while.51 = (s32[]{:T(128)}, f32[1,16,16,512]{3,2,1,0:T(8,128)S(1)}, f32[16,512]{1,0:T(8,128)S(1)}, f32[1,16,16,512]{3,2,1,0:T(8,128)S(1)}, s32[]{:T(128)}) while((s32[]{:T(128)}, f32[1,16,16,512]{3,2,1,0:T(8,128)S(1)}, f32[16,512]{1,0:T(8,128)S(1)}, f32[1,16,16,512]{3,2,1,0:T(8,128)S(1)}, s32[]{:T(128)}) %tuple.127), condition=%wide.region_8.9_spmd, body=%wide.region_7.8_spmd.sunk | while | flops 262146 | bytes 3702885 | solution.py:118
  658.6 11.4 collective-permute-done.1
  684.7 11.4 collective-permute-done.1
  710.8 11.4 collective-permute-done.1
  736.9 11.4 collective-permute-done.1
  775.8 10.7 collective-permute-done.1
  1074.2 10.8 fusion.51
  1094.9 10.9 fusion.13
  1119.3 11.2 fusion.15
  1158.0 27.9 %reduce_sum.28 = f32[3,7,8192]{2,0,1:T(4,128)} reduce(f32[1,128,3,7,8192]{4,1,2,3,0:T(8,128)} %fusion.25, f32[]{:T(128)} %constant.65.clone.1), dimensions={0,1}, to_apply=%region_9.10 | reduce | flops 21848064 | bytes 88768512 | tf_op jit(solution)/shard_map/reduce_sum | solution.py:105
  1186.0 142.0 %psum.30 = f32[8192]{0:T(1024)S(1)} all-reduce(f32[8192]{0:T(1024)S(1)} %copy-done.25), channel_id=1, replica_groups=mesh['dp'=4,'ctx'=32] {'ctx'}, use_global_device_ids=true, to_apply=%region_13.14 | all-reduce | flops 8192 | bytes 65536 | tf_op jit(solution)/shard_map/psum | solution.py:161
  1328.1 14.7 %psum.31 = f32[8192]{0:T(1024)} all-reduce(f32[8192]{0:T(1024)S(1)} %psum.30), channel_id=1, replica_groups=mesh['dp'=4,'ctx'=32] {'dp'}, use_global_device_ids=true, to_apply=%region_14.15 | all-reduce | flops 8192 | bytes 65536 | tf_op jit(solution)/shard_map/psum | solution.py:161
  1353.1 34.2 %fusion.27 = bf16[1,128,3,8192]{3,1,2,0:T(8,128)(2,1)} fusion(f32[1,134,3,8192]{3,1,2,0:T(8,128)} %pad_maximum_fusion, f32[3,8192]{1,0:T(4,128)S(1)} %copy-done.13, f32[3,8192]{1,0:T(4,128)S(1)} %copy-done.15, f32[3,8192]{1,0:T(4,128)S(1)} %copy-done.17, f32[3,8192]{1,0:T(4,128)S(1)} %copy-done.19, f32[3,8192]{1,0:T(4,128)S(1)} %copy-done.21, ...), kind=kLoop, calls=%fused_computation.55 | loop fusion | flops 50331648 | bytes 95059968 | tf_op jit(solution)/shard_map/convert_element_type | solution.py:158
  (318 shorter events, 911.8 us)
Async XLA Ops:
  7.2 1335.6 %all-reduce.3.cloned.1.call-start = ((), (), s32[]{:S(2)}) async-start(), calls=%async_computation | async-start | bytes 1835008 | tf_op jit(solution)/shard_map/psum | solution.py:161
  8.3 58.7 %collective-permute-start.2 = (bf16[1,6,3,8192]{3,1,2,0:T(8,128)(2,1)S(1)}, bf16[1,6,3,8192]{3,1,2,0:T(8,128)(2,1)S(1)}, u32[]{:S(2)}, u32[]{:S(2)}) collective-permute-start(bf16[1,6,3,8192]{3,1,2,0:T(8,128)(2,1)S(1)} %slice.87), channel_id=1, source_target_pairs={{0,1},{1,2},{2,3},{3,4},{4,5},{5,6},{6,7},{7,8},{8,9},{9,10},{10,1... | collective-permute-start | bytes 884744 | tf_op jit(solution)/shard_map/ppermute | solution.py:13
  382.3 12.6 collective-permute-start
  395.1 12.6 collective-permute-start
  407.8 12.6 collective-permute-start
  420.5 12.6 collective-permute-start
  433.2 12.6 collective-permute-start
  446.0 12.6 collective-permute-start
  458.7 12.6 collective-permute-start
  471.4 12.6 collective-permute-start
  484.1 12.6 collective-permute-start
  496.9 12.6 collective-permute-start
  509.6 12.6 collective-permute-start
  522.3 12.6 collective-permute-start
  656.7 13.4 collective-permute-start.1
  682.8 13.4 collective-permute-start.1
  708.9 13.4 collective-permute-start.1
  734.9 13.4 collective-permute-start.1
  748.4 12.6 collective-permute-start.1
  773.9 12.6 collective-permute-start.1
  799.3 12.6 collective-permute-start.1
  812.1 12.6 collective-permute-start.1
  1117.0 225.8 %collective-permute-start.3 = (f32[1,6,3,8192]{3,0,2,1:T(1,128)S(1)}, f32[1,6,3,8192]{3,0,2,1:T(1,128)S(1)}, u32[]{:S(2)}, u32[]{:S(2)}) collective-permute-start(f32[1,6,3,8192]{3,0,2,1:T(1,128)S(1)} %copy.74), channel_id=1, source_target_pairs={{1,0},{2,1},{3,2},{4,3},{5,4},{6,5},{7,6},{8,7},{9,8},{10,9},{11,1... | collective-permute-start | bytes 1769480 | tf_op jit(solution)/shard_map/ppermute | solution.py:13
  1186.0 203.9 %all-reduce.5.cloned.1.call-start = ((), (), s32[]{:S(2)}) async-start(), calls=%async_computation.1 | async-start | bytes 1835008 | tf_op jit(solution)/shard_map/psum | solution.py:161
  (70 other events, 911.8 us)
Sparse Core Ops, SparseCore 0:
  1186.1 140.2 all-reduce.2
  1342.9 46.9 all-reduce.4
